TPU v7x, 32 devices: a whole 2x2x4 slice. The times are simulated.
32 devices in a mesh: kvh: 2 (over x), ctx: 16 (over z, y, core).
Axes of the slice: x: 2, y: 2, z: 4, core: 2. Of those that a mesh axis runs over, the one named last changes fastest.
Arguments:
- queries: bfloat16 [512, 32, 128], P('ctx', 'kvh'), parts along dimension 1, may hold values from -6 to 6
- cache_keys: bfloat16 [16384, 256], P('ctx', 'kvh'), parts along dimension 1, may hold values from -6 to 6
- cache_values: bfloat16 [16384, 256], P('ctx', 'kvh'), parts along dimension 1, may hold values from -6 to 6
- span_offset: int32 [1], replicated, may hold values from 0 to 8191
- positions: int32 [512], replicated, may hold values from 0 to 8191
Outputs:
- attended: bfloat16 [512, 32, 128], P('ctx', 'kvh'), parts along dimension 1
There are 2 independent parts, one for each index of `kvh`. A program takes and returns all parts, laid end to end along the dimension named above; an argument that names none is the same for every part. Nothing has to cross between parts.
All inputs are finite; a program needn't handle non-finite values.
Results may differ from a plain program's by a relative error of at most 0.0029.
Values may be sent and summed in bfloat16 or wider, within the bound.
No kernel may reach another device: no remote copies, remote signals or barrier semaphores. Data moves between devices by JAX's collectives and lax.ppermute only.
A program may use at most 64 MiB of HBM per device.

v0:
```python
import jax
import jax.numpy as jnp
from jax import lax
from jax.sharding import PartitionSpec as P

masked_floor = -1e30


def local(queries, cache_keys, cache_values, span_offset, positions):
    gathered = lax.all_gather(queries, "ctx", axis=0, tiled=True)
    token_count, head_count, head_width = gathered.shape
    row_count = token_count * head_count
    shard_keys = cache_keys.shape[0]
    key_start = lax.axis_index("ctx") * shard_keys
    key_position = key_start + lax.iota(jnp.int32, shard_keys)
    row_limit = jnp.repeat(span_offset[0] + positions, head_count)
    row_block = 512
    block_count = row_count // row_block
    query_blocks = gathered.reshape(block_count, row_block, head_width)
    limit_blocks = row_limit.reshape(block_count, row_block)
    score_scale = head_width ** (-0.5)

    def shard_partial(inputs):
        query_block, limit_block = inputs
        scores = (
            lax.dot_general(
                query_block,
                cache_keys,
                (((1,), (1,)), ((), ())),
                preferred_element_type=jnp.float32,
            )
            * score_scale
        )
        visible = key_position[None, :] <= limit_block[:, None]
        shard_max = jnp.max(jnp.where(visible, scores, masked_floor), axis=1)
        weights = jnp.where(visible, jnp.exp(scores - shard_max[:, None]), 0.0).astype(jnp.bfloat16)
        shard_den = jnp.sum(weights.astype(jnp.float32), axis=1)
        shard_num = jnp.dot(weights, cache_values, preferred_element_type=jnp.float32)
        return (shard_num, shard_max, shard_den)

    numerator, local_max, denominator = lax.map(shard_partial, (query_blocks, limit_blocks))
    numerator = numerator.reshape(token_count, head_count * head_width)
    local_max = local_max.reshape(token_count, head_count)
    denominator = denominator.reshape(token_count, head_count)
    got_num, got_max, got_den = (
        lax.all_to_all(numerator[None], "ctx", split_axis=1, concat_axis=0, tiled=True),
        lax.all_to_all(local_max[None], "ctx", split_axis=1, concat_axis=0, tiled=True),
        lax.all_to_all(denominator[None], "ctx", split_axis=1, concat_axis=0, tiled=True),
    )
    row_top = jnp.max(got_max, axis=0)
    factor = jnp.exp(got_max - row_top[None])
    sources, own_tokens = (got_max.shape[0], got_max.shape[1])
    num_sum = jnp.sum(
        got_num.reshape(sources, own_tokens, head_count, head_width) * factor[:, :, :, None], axis=0
    )
    den_sum = jnp.sum(got_den * factor, axis=0)
    attended = num_sum / den_sum[:, :, None]
    return attended.astype(jnp.bfloat16)


def solution(mesh):
    in_specs = (P("ctx", "kvh", None), P("ctx", "kvh"), P("ctx", "kvh"), P(), P())
    out_specs = P("ctx", "kvh", None)
    return jax.shard_map(local, mesh=mesh, in_specs=in_specs, out_specs=out_specs, check_vma=False)
```

profile of v0, /device:TPU:13, one launch (start us, length us, event | category | flops | bytes accessed | tf_op | source)
XLA Modules:
  0.0 250.9 jit_solution(5904179462942185829)
XLA Ops:
  9.0 41.5 %all-gather.2.cloned.1.call-done = bf16[512,16,128]{2,1,0:T(8,128)(2,1)} async-done(((bf16[32,16,128]{2,1,0:T(8,128)(2,1)}), bf16[512,16,128]{2,1,0:T(8,128)(2,1)}) %all-gather.2.cloned.1.call-update) | async-done | bytes 2097168 | tf_op jit(solution)/shard_map/all_gather | solution.py:10
  50.5 59.1 %while.15 = (s32[]{:T(128)}, f32[16,512,128]{2,1,0:T(8,128)}, f32[16,512]{1,0:T(8,128)S(1)}, f32[16,512]{1,0:T(8,128)S(1)}, s32[16,512]{1,0:T(8,128)S(1)}, /*ind...) while((s32[]{:T(128)}, f32[16,512,128]{2,1,0:T(8,128)}, ...), condition=%wide.region_3.4_spmd.clone, body=%wide.region_0.3_spmd.clone.sunk | while | flops 274202624 | bytes 8292521 | solution.py:41
  50.5 1.6 fusion.22
  54.2 1.6 fusion.22
  57.9 1.6 fusion.22
  61.6 1.6 fusion.22
  65.3 1.6 fusion.22
  67.8 1.2 fusion.23
  69.0 1.6 fusion.22
  71.5 1.2 fusion.23
  72.7 1.6 fusion.22
  76.4 1.6 fusion.22
  80.1 1.6 fusion.22
  82.6 1.2 fusion.23
  83.8 1.6 fusion.22
  87.5 1.6 fusion.22
  91.1 1.6 fusion.22
  93.7 1.2 fusion.23
  94.8 1.6 fusion.22
  97.4 1.2 fusion.23
  98.5 1.6 fusion.22
  102.2 1.6 fusion.22
  105.9 1.6 fusion.22
  110.2 1.2 reduce.1
  112.2 5.7 %all-to-all-start.2 = ((f32[16,1,512]{2,1,0:T(1,128)}), f32[16,1,512]{2,1,0:T(1,128)S(1)}, u32[]{:S(2)}, u32[]{:S(2)}) async-start(f32[16,1,512]{2,1,0:T(1,128)} %reshape.55), calls=%async_computation.2 | async-start | bytes 65536 | tf_op jit(solution)/shard_map/all_to_all | solution.py:48
  118.1 1.2 reduce.3
  119.4 2.7 %all-to-all-done.2 = f32[16,1,512]{2,1,0:T(1,128)S(1)} async-done(((f32[16,1,512]{2,1,0:T(1,128)}), f32[16,1,512]{2,1,0:T(1,128)S(1)}, u32[]{:S(2)}, u32[]{:S(2)}) %all-to-all-start.2) | async-done | bytes 32800 | tf_op jit(solution)/shard_map/all_to_all | solution.py:48
  122.1 9.2 %all_to_all.36 = f32[16,1,512]{2,1,0:T(1,128)S(1)} all-to-all(f32[16,1,512]{2,1,0:T(1,128)S(1)} %reshape.53), channel_id=1, replica_groups=mesh['kvh'=2,'ctx'=16] {'ctx'}, dimensions={0} | all-to-all | bytes 65536 | tf_op jit(solution)/shard_map/all_to_all | solution.py:47
  131.3 6.8 %all-to-all-start = ((f32[1,512,2048]{2,0,1:T(1,128)}), f32[1,512,2048]{2,0,1:T(1,128)}, u32[]{:S(2)}, u32[]{:S(2)}) async-start(f32[1,512,2048]{2,0,1:T(1,128)} %bitcast.51), calls=%async_computation | async-start | bytes 8388608 | tf_op jit(solution)/shard_map/all_to_all | solution.py:46
  140.6 90.1 %all-to-all-done = f32[1,512,2048]{2,0,1:T(1,128)} async-done(((f32[1,512,2048]{2,0,1:T(1,128)}), f32[1,512,2048]{2,0,1:T(1,128)}, u32[]{:S(2)}, u32[]{:S(2)}) %all-to-all-start) | async-done | bytes 4194336 | tf_op jit(solution)/shard_map/all_to_all | solution.py:46
  230.7 2.5 %mul.33 = f32[16,32,16,128]{3,2,1,0:T(8,128)} broadcast(f32[16,32,16]{2,1,0:T(8,128)S(1)} %get-tuple-element.99), dimensions={0,1,2} | broadcast | bytes 4227072 | tf_op jit(solution)/shard_map/mul | solution.py:54
  233.2 10.0 %multiply_reduce_fusion = f32[32,2048]{1,0:T(8,128)S(1)} fusion(f32[1,16,32,2048]{3,0,2,1:T(1,128)} %bitcast.3, f32[1,16,32,2048]{3,0,2,1:T(1,128)} %bitcast.50), kind=kLoop, calls=%fused_computation.14 | loop fusion | flops 2031616 | bytes 8650752 | tf_op jit(solution)/shard_map/reduce_sum | solution.py:53
  (145 shorter events, 34.2 us)
Async XLA Ops:
  6.5 44.0 %all-gather.2.cloned.1.call-start = ((), (), s32[]{:S(2)}) async-start(), calls=%async_computation.3 | async-start | bytes 2228224 | tf_op jit(solution)/shard_map/all_gather | solution.py:10
  52.1 1.0 copy-start
  55.8 1.0 copy-start
  59.5 1.0 copy-start
  63.2 1.0 copy-start
  66.9 1.0 copy-start
  70.6 1.0 copy-start
  74.3 1.0 copy-start
  77.9 1.0 copy-start
  81.6 1.0 copy-start
  85.3 1.0 copy-start
  89.0 1.0 copy-start
  92.7 1.0 copy-start
  96.4 1.0 copy-start
  100.1 1.0 copy-start
  103.8 1.0 copy-start
  107.5 1.0 copy-start
  112.2 9.9 %all-to-all-start.2 = ((f32[16,1,512]{2,1,0:T(1,128)}), f32[16,1,512]{2,1,0:T(1,128)S(1)}, u32[]{:S(2)}, u32[]{:S(2)}) async-start(f32[16,1,512]{2,1,0:T(1,128)} %reshape.55), calls=%async_computation.2 | async-start | bytes 65536 | tf_op jit(solution)/shard_map/all_to_all | solution.py:48
  131.3 99.3 %all-to-all-start = ((f32[1,512,2048]{2,0,1:T(1,128)}), f32[1,512,2048]{2,0,1:T(1,128)}, u32[]{:S(2)}, u32[]{:S(2)}) async-start(f32[1,512,2048]{2,0,1:T(1,128)} %bitcast.51), calls=%async_computation | async-start | bytes 8388608 | tf_op jit(solution)/shard_map/all_to_all | solution.py:46
Sparse Core Ops, SparseCore 0:
  9.5 40.9 all-gather.1
where the time goes:
time: 252 us; the launch traced here: 251 us
  waiting for transfers between devices  135 us (54%)
  matrix products  43.6 us (17%)
  other arithmetic  26.8 us (11%)
  between operations  14.2 us (6%)
  starting transfers between devices  12.6 us (5%)
  blocking collectives  9.19 us (4%)
  local copies, waits for them, and re-layouts  9.16 us (4%)
    all_to_all x1, waiting for transfers between devices, local(): lax.all_to_all(numerator[None], 'ctx', split_axis=1, concat_axis=0, tiled...  90.1 us
    all_gather x1, waiting for transfers between devices, local(): gathered = lax.all_gather(queries, 'ctx', axis=0, tiled=True)  41.5 us
    dot_general x16, matrix products, shard_partial(): lax.dot_general(query_block, cache_keys, (((1,), (1,)), ((), ())), prefer...  25.2 us
    dot_general x16, matrix products, shard_partial(): jnp.dot(weights, cache_values, preferred_element_type=jnp.float32)  18.4 us
    reduce_sum x16, other arithmetic, shard_partial(): shard_den = jnp.sum(weights.astype(jnp.float32), axis=1)  11.4 us
    reduce_sum x1, other arithmetic, local(): jnp.sum(got_num.reshape(sources, own_tokens, head_count, head_width) * fa...  10 us
    all_to_all x1, blocking collectives, local(): lax.all_to_all(local_max[None], 'ctx', split_axis=1, concat_axis=0, tiled...  9.19 us
    all_to_all x1, starting transfers between devices, local(): lax.all_to_all(numerator[None], 'ctx', split_axis=1, concat_axis=0, tiled...  6.85 us
  transfers between devices with their start and end apart: 3, of which 3 were waited for; matrix products, arithmetic and copies ran while one was open for 2% of the time, Pallas kernels for 0%

commit v1 on v0

--- a/solution.py
+++ b/solution.py
@@ -43,7 +43,12 @@
     local_max = local_max.reshape(token_count, head_count)
     denominator = denominator.reshape(token_count, head_count)
     got_num, got_max, got_den = (
-        lax.all_to_all(numerator[None], "ctx", split_axis=1, concat_axis=0, tiled=True),
+        jnp.concatenate(
+            lax.all_to_all(
+                jnp.stack(jnp.split(numerator[None], lax.axis_size("ctx"), axis=1)), "ctx", 0, 0
+            ),
+            axis=0,
+        ),
         lax.all_to_all(local_max[None], "ctx", split_axis=1, concat_axis=0, tiled=True),
         lax.all_to_all(denominator[None], "ctx", split_axis=1, concat_axis=0, tiled=True),
     )

time: 252 us -> 273 us (1.083)
  local copies, waits for them, and re-layouts: 9.16 us -> 44.8 us
  blocking collectives: 9.19 us -> 0 us
  waiting for transfers between devices: 135 us -> 127 us
  starting transfers between devices: 12.6 us -> 18.4 us
  other arithmetic: 26.8 us -> 21.4 us
    unnamed x6 -> x21, local copies, waits for them, and re-layouts: 2.42 us -> 28.3 us
    all_to_all x1 -> x0, blocking collectives: 9.19 us -> none  [local(): lax.all_to_all(local_max[None], 'ctx', split_axis=1, concat_axis=0, tiled...]
    all_to_all x1 -> x2, waiting for transfers between devices: 90.1 us -> 82.7 us  [the longest x1 82.3 us: local(): lax.all_to_all(jnp.stack(jnp.split(numerator[None], lax.axis_size('ctx'),...]
    another operation x0 -> x2, local copies, waits for them, and re-layouts: none -> 6.56 us  [the longest x1 4.88 us: local(): numerator[None]]
    reduce_sum x1, other arithmetic: 10 us -> 4.05 us  [local(): jnp.sum(got_num.reshape(sources, own_tokens, head_count, head_width) * fa...]
    all_to_all x1 -> x2, starting transfers between devices: 6.85 us -> 12.6 us  [the longest x1 6.85 us: local(): lax.all_to_all(jnp.stack(jnp.split(numerator[None], lax.axis_size('ctx'),...]
    mul x1 -> x2, local copies, waits for them, and re-layouts: 2.53 us -> 7.5 us  [local(): got_num.reshape(sources, own_tokens, head_count, head_width)]
  transfers between devices with their start and end apart: 3 -> 4, of which waited for: 3 -> 4; matrix products, arithmetic and copies ran while one was open for 2% -> 6% of each run, Pallas kernels for 0% -> 0%
where the time goes in v1:
time: 273 us; the launch traced here: 271 us
  waiting for transfers between devices  127 us (47%)
  local copies, waits for them, and re-layouts  44.8 us (16%)
  matrix products  44.1 us (16%)
  other arithmetic  21.4 us (8%)
  starting transfers between devices  18.4 us (7%)
  between operations  14.2 us (5%)
    all_to_all x1, waiting for transfers between devices, local(): lax.all_to_all(jnp.stack(jnp.split(numerator[None], lax.axis_size('ctx'),...  82.3 us
    all_gather x1, waiting for transfers between devices, local(): gathered = lax.all_gather(queries, 'ctx', axis=0, tiled=True)  41.5 us
    unnamed x21, local copies, waits for them, and re-layouts  28.3 us
    dot_general x16, matrix products, shard_partial(): lax.dot_general(query_block, cache_keys, (((1,), (1,)), ((), ())), prefer...  25.6 us
    dot_general x16, matrix products, shard_partial(): jnp.dot(weights, cache_values, preferred_element_type=jnp.float32)  18.5 us
    reduce_sum x16, other arithmetic, shard_partial(): shard_den = jnp.sum(weights.astype(jnp.float32), axis=1)  11.5 us
    mul x2, local copies, waits for them, and re-layouts, local(): got_num.reshape(sources, own_tokens, head_count, head_width)  7.5 us
    all_to_all x1, starting transfers between devices, local(): lax.all_to_all(jnp.stack(jnp.split(numerator[None], lax.axis_size('ctx'),...  6.85 us
  transfers between devices with their start and end apart: 4, of which 4 were waited for; matrix products, arithmetic and copies ran while one was open for 6% of the time, Pallas kernels for 0%

profile of v1, /device:TPU:13, one launch (start us, length us, event | category | flops | bytes accessed | tf_op | source)
XLA Modules:
  0.0 271.2 jit_solution(17165158210022789043)
XLA Ops:
  9.0 41.5 %all-gather.2.cloned.1.call-done = bf16[512,16,128]{2,1,0:T(8,128)(2,1)} async-done(((bf16[32,16,128]{2,1,0:T(8,128)(2,1)}), bf16[512,16,128]{2,1,0:T(8,128)(2,1)}) %all-gather.2.cloned.1.call-update) | async-done | bytes 2097168 | tf_op jit(solution)/shard_map/all_gather | solution.py:10
  50.5 58.4 %while.15 = (s32[]{:T(128)}, f32[16,512,128]{2,1,0:T(8,128)}, f32[16,512]{1,0:T(8,128)S(1)}, f32[16,512]{1,0:T(8,128)S(1)}, s32[16,512]{1,0:T(8,128)S(1)}, /*ind...) while((s32[]{:T(128)}, f32[16,512,128]{2,1,0:T(8,128)}, ...), condition=%wide.region_3.4_spmd.clone, body=%wide.region_0.3_spmd.clone.sunk | while | flops 274202624 | bytes 8293529 | solution.py:41
  50.6 1.6 fusion.38
  57.8 1.6 fusion.38
  61.5 1.6 fusion.38
  79.8 1.6 fusion.38
  83.4 1.6 fusion.38
  108.9 4.9 %broadcast_in_dim_reshape.9 = f32[1,512,2048]{2,1,0:T(8,128)} reshape(f32[16,512,128]{2,1,0:T(8,128)} %get-tuple-element.54) | data formatting | bytes 8388608 | tf_op jit(solution)/shard_map/broadcast_in_dim;reshape | solution.py:48
  113.8 1.7 fusion.25
  115.5 1.7 fusion.24
  117.1 1.7 fusion.23
  118.8 1.7 fusion.22
  120.5 1.7 fusion.21
  122.2 1.7 fusion.20
  123.9 1.7 fusion.19
  125.6 1.7 fusion.18
  127.2 1.7 fusion.17
  128.9 1.7 fusion.16
  130.6 1.7 fusion.15
  132.3 1.7 fusion.14
  134.0 1.7 fusion.13
  135.6 1.7 fusion.12
  140.1 5.7 %all-to-all-start.1 = ((f32[16,1,512]{2,1,0:T(1,128)}), f32[16,1,512]{2,1,0:T(1,128)S(1)}, u32[]{:S(2)}, u32[]{:S(2)}) async-start(f32[16,1,512]{2,1,0:T(1,128)} %reshape.31), calls=%async_computation.1 | async-start | bytes 65536 | tf_op jit(solution)/shard_map/all_to_all | solution.py:52
  145.8 1.7 fusion.11
  150.0 5.9 %all-to-all-start.2 = ((f32[16,1,512]{2,1,0:T(1,128)}), f32[16,1,512]{2,1,0:T(1,128)S(1)}, u32[]{:S(2)}, u32[]{:S(2)}) async-start(f32[16,1,512]{2,1,0:T(1,128)} %reshape.33), calls=%async_computation.2 | async-start | bytes 65536 | tf_op jit(solution)/shard_map/all_to_all | solution.py:53
  155.9 1.7 fusion.10
  157.6 2.5 all-to-all-done.2
  160.1 6.9 %all-to-all-start = ((f32[16,1,32,2048]{3,2,1,0:T(8,128)}), f32[16,1,32,2048]{3,2,1,0:T(8,128)}, u32[]{:S(2)}, u32[]{:S(2)}) async-start(f32[16,1,32,2048]{3,2,1,0:T(8,128)} %fusion.10), calls=%async_computation | async-start | bytes 8388608 | tf_op jit(solution)/shard_map/all_to_all | solution.py:47
  169.6 2.6 mul.24
  172.2 4.9 %mul.25 = f32[16,1,32,2048]{3,2,1,0:T(8,128)} reshape(f32[16,32,16,128]{3,2,1,0:T(8,128)} %mul.24) | data formatting | bytes 8388608 | tf_op jit(solution)/shard_map/mul | solution.py:59
  177.1 82.3 %all-to-all-done = f32[16,1,32,2048]{3,2,1,0:T(8,128)} async-done(((f32[16,1,32,2048]{3,2,1,0:T(8,128)}), f32[16,1,32,2048]{3,2,1,0:T(8,128)}, u32[]{:S(2)}, u32[]{:S(2)}) %all-to-all-start) | async-done | bytes 4194336 | tf_op jit(solution)/shard_map/all_to_all | solution.py:47
  259.5 4.1 %multiply_reduce_fusion = f32[32,2048]{1,0:T(8,128)S(1)} fusion(f32[16,1,32,2048]{3,2,1,0:T(8,128)} %all-to-all-done, f32[16,1,32,2048]{3,2,1,0:T(8,128)} %mul.25), kind=kLoop, calls=%fused_computation.14 | loop fusion | flops 2031616 | bytes 8650752 | tf_op jit(solution)/shard_map/reduce_sum | solution.py:58
  (164 shorter events, 60.0 us)
Async XLA Ops:
  6.5 44.0 %all-gather.2.cloned.1.call-start = ((), (), s32[]{:S(2)}) async-start(), calls=%async_computation.3 | async-start | bytes 2228224 | tf_op jit(solution)/shard_map/all_gather | solution.py:10
  50.5 2.3 copy-start
  54.1 2.4 copy-start
  57.8 2.4 copy-start
  61.5 2.4 copy-start
  65.1 2.4 copy-start
  68.8 2.4 copy-start
  72.4 2.4 copy-start
  76.1 2.4 copy-start
  79.7 2.4 copy-start
  83.4 2.4 copy-start
  87.0 2.4 copy-start
  90.7 2.4 copy-start
  94.3 2.4 copy-start
  98.0 2.4 copy-start
  101.6 2.4 copy-start
  105.3 2.4 copy-start
  140.1 9.9 %all-to-all-start.1 = ((f32[16,1,512]{2,1,0:T(1,128)}), f32[16,1,512]{2,1,0:T(1,128)S(1)}, u32[]{:S(2)}, u32[]{:S(2)}) async-start(f32[16,1,512]{2,1,0:T(1,128)} %reshape.31), calls=%async_computation.1 | async-start | bytes 65536 | tf_op jit(solution)/shard_map/all_to_all | solution.py:52
  150.0 10.1 %all-to-all-start.2 = ((f32[16,1,512]{2,1,0:T(1,128)}), f32[16,1,512]{2,1,0:T(1,128)S(1)}, u32[]{:S(2)}, u32[]{:S(2)}) async-start(f32[16,1,512]{2,1,0:T(1,128)} %reshape.33), calls=%async_computation.2 | async-start | bytes 65536 | tf_op jit(solution)/shard_map/all_to_all | solution.py:53
  160.1 99.3 %all-to-all-start = ((f32[16,1,32,2048]{3,2,1,0:T(8,128)}), f32[16,1,32,2048]{3,2,1,0:T(8,128)}, u32[]{:S(2)}, u32[]{:S(2)}) async-start(f32[16,1,32,2048]{3,2,1,0:T(8,128)} %fusion.10), calls=%async_computation | async-start | bytes 8388608 | tf_op jit(solution)/shard_map/all_to_all | solution.py:47
Sparse Core Ops, SparseCore 0:
  9.5 40.9 all-gather.1
